TPU v7x, 256 devices: a whole 4x4x8 slice. The times are simulated.
256 devices in a mesh: col: 8 (over z_lo, core), dp: 32 (over z_hi, y, x).
Axes of the slice: x: 4, y: 4, z: 8 (z_hi: 2, z_lo: 4; z = z_hi * 4 + z_lo), core: 2. Of those that a mesh axis runs over, the one named last changes fastest.
Arguments:
- acts: bfloat16 [12288, 5120], P('dp', 'col'), may hold values from -6 to 6
- out_grad: bfloat16 [12288, 8192], P('dp', 'col'), may hold values from -6 to 6
- projection: bfloat16 [5120, 256], replicated, may hold values from -0.078125 to 0.078125
- weight: bfloat16 [5120, 8192], P('dp', 'col'), may hold values from -0.078125 to 0.078125
- m_codes: int32 [256, 8192], P('dp', 'col'), may hold values from -127 to 127
- m_exps: int32 [256, 256], P('dp', 'col'), may hold values from -16 to -9
- v_codes: int32 [256, 8192], P('dp', 'col'), may hold values from 1 to 127
- v_exps: int32 [256, 256], P('dp', 'col'), may hold values from -24 to -18
- next_acts: bfloat16 [12288, 5120], P('dp', 'col'), may hold values from -6 to 6
Outputs:
- next_out: bfloat16 [12288, 8192], P('dp', 'col')
- new_weight: bfloat16 [5120, 8192], P('dp', 'col')
- update: float32 [256, 8192], P('dp', 'col')
Inputs may be any that keep to these rules, and one draw needn't show every extreme that they name: `v_codes`: second moment mantissas are positive.
All inputs are finite; a program needn't handle non-finite values.
Results may differ from a plain program's by a relative error of at most 0.0051.
Values may be sent and summed in bfloat16 or wider, within the bound.
No kernel may reach another device: no remote copies, remote signals or barrier semaphores. Data moves between devices by JAX's collectives and lax.ppermute only.
A program may use at most 128 MiB of HBM per device.

v0:
```python
import jax
import jax.numpy as jnp
from jax import lax
from jax.sharding import Mesh
from jax.sharding import PartitionSpec as P

DP = ("dp_0", "dp_1", "dp_2")
learn_rate = 0.02
beta_one = 0.9
beta_two = 0.999
epsilon = 1e-08
correct_first = 0.9999734386011124
correct_second = 0.0952078528862904


def sent_to_all(shard, axis):
    size = lax.axis_size(axis)
    return lax.all_to_all(
        jnp.broadcast_to(shard[None], (size, *shard.shape)), axis, 0, 0, tiled=True
    )


def over_copies(shard, axis):
    everything = sent_to_all(shard, axis)
    return jnp.sum(everything, axis=0)


def cut_along(shard, dim, size):
    shape = shard.shape
    pieces = shard.reshape(*shape[:dim], size, shape[dim] // size, *shape[dim + 1 :])
    return jnp.moveaxis(pieces, dim, 0)


def sum_at_owner(shard, axis, dim):
    pieces = cut_along(shard, dim, lax.axis_size(axis))
    arrived = lax.all_to_all(pieces, axis, split_axis=0, concat_axis=0, tiled=True)
    return arrived.sum(axis=0)


def joined_along(pieces, dim):
    shape = list(pieces.shape[1:])
    shape[dim] *= pieces.shape[0]
    return jnp.moveaxis(pieces, 0, dim).reshape(shape)


def gather_in_order(shard, axes, sequence):
    pieces = shard[None]
    for k in sequence:
        pieces = lax.all_gather(pieces, axes[k], axis=0, tiled=True)
    block = [lax.axis_size(axes[k]) for k in reversed(sequence)]
    pieces = pieces.reshape(*block, *shard.shape)
    turned = sorted(range(len(sequence)), key=lambda place: sequence[len(sequence) - 1 - place])
    return pieces.transpose(*turned, *range(len(sequence), pieces.ndim)).reshape(-1, *shard.shape)


def gathered_by_axis(shard, axes, sequence, dim):
    return joined_along(gather_in_order(shard, axes, sequence), dim)


def collect(shard, axis, dim):
    pieces = sent_to_all(shard, axis)
    return joined_along(pieces, dim)


def decode(codes, exps):
    scale = jnp.exp2(exps.astype(jnp.float32))
    rows = codes.shape[0]
    values = (codes.astype(jnp.float32) / 128.0).reshape(
        rows, exps.shape[1], codes.shape[1] // exps.shape[1]
    )
    return (values * scale[:, :, None]).reshape(rows, codes.shape[1])


def body(acts, out_grad, projection, weight, m_codes, m_exps, v_codes, v_exps, next_acts):
    col_width = acts.shape[1]
    col_start = lax.axis_index("col") * col_width
    proj_cols = lax.dynamic_slice_in_dim(projection, col_start, col_width, 0)
    partial_value = jnp.dot(acts, proj_cols, preferred_element_type=jnp.float32)
    lowrank = over_copies(partial_value, "col").astype(jnp.bfloat16)
    tokens_all = acts.shape[0] * lax.axis_size(DP)
    grad = (
        sum_at_owner(
            lax.dot_general(
                lowrank, out_grad, (((0,), (0,)), ((), ())), preferred_element_type=jnp.float32
            ),
            DP,
            0,
        )
        / tokens_all
    )
    m_old = decode(m_codes, m_exps)
    v_old = decode(v_codes, v_exps)
    first = beta_one * m_old + (1.0 - beta_one) * grad
    second = beta_two * v_old + (1.0 - beta_two) * grad * grad
    update = first / correct_first / (jnp.sqrt(second / correct_second) + epsilon)
    direction = update.astype(jnp.bfloat16)
    full_next = lax.all_gather(next_acts, "col", axis=1, tiled=True)
    row_count = weight.shape[0]
    row_start = lax.axis_index(DP) * row_count
    old_full = gathered_by_axis(weight, DP, (0, 1, 2), 0)
    dir_full = collect(direction, DP, 0)
    delta_full = jnp.dot(projection, dir_full, preferred_element_type=jnp.float32)
    full_weight = (old_full.astype(jnp.float32) - learn_rate * delta_full).astype(jnp.bfloat16)
    new_weight = lax.dynamic_slice_in_dim(full_weight, row_start, row_count, 0)
    result = jnp.dot(full_next, full_weight, preferred_element_type=jnp.float32)
    return (result.astype(jnp.bfloat16), new_weight, update)


def solution(mesh):
    torus = Mesh(mesh.devices.reshape(mesh.shape["col"], 2, 4, 4), ("col", "dp_0", "dp_1", "dp_2"))
    return jax.shard_map(
        body,
        mesh=torus,
        in_specs=(
            P(DP, "col"),
            P(DP, "col"),
            P(),
            P(DP, "col"),
            P(DP, "col"),
            P(DP, "col"),
            P(DP, "col"),
            P(DP, "col"),
            P(DP, "col"),
        ),
        out_specs=(P(DP, "col"), P(DP, "col"), P(DP, "col")),
        check_vma=False,
    )
```

profile of v0, /device:TPU:2, one launch (start us, length us, event | category | flops | bytes accessed | tf_op | source)
XLA Modules:
  0.0 285.9 jit_solution(1275187251293601851)
XLA Ops:
  7.2 0.0 all-gather.5.cloned.1.call-start
  7.2 21.9 %all-gather = bf16[320,1024]{1,0:T(8,128)(2,1)} all-gather(bf16[160,1024]{1,0:T(8,128)(2,1)} %param.12), channel_id=2, replica_groups=mesh['col'=8,'dp_0'=2,'dp_1'=4,'dp_2'=4] {'dp_0'}, dimensions={0}, use_global_device_ids=true | all-gather | bytes 983040 | tf_op jit(solution)/shard_map/all_gather | solution.py:49
  29.2 0.0 all-gather.7.cloned.1.call-start
  29.2 39.9 %all-gather.5.cloned.1.call-done = bf16[8,160,1024]{2,1,0:T(8,128)(2,1)} async-done(((bf16[2,160,1024]{2,1,0:T(8,128)(2,1)}), bf16[8,160,1024]{2,1,0:T(8,128)(2,1)}) %all-gather.5.cloned.1.call-update) | async-done | bytes 2621456 | tf_op jit(solution)/shard_map/all_gather | solution.py:49
  69.2 1.4 convolution_bitcast_fusion.1
  70.6 0.2 copy.26
  70.8 2.0 broadcast_in_dim.7
  72.8 4.9 %all-to-all-start = ((f32[8,384,256]{2,1,0:T(8,128)}), f32[8,384,256]{2,1,0:T(8,128)}, u32[]{:S(2)}, u32[]{:S(2)}) async-start(f32[8,384,256]{2,1,0:T(8,128)} %broadcast_in_dim.7), calls=%async_computation | async-start | bytes 6291456 | tf_op jit(solution)/shard_map/all_to_all | solution.py:18
  77.7 0.0 all-gather.9.cloned.1.call-start
  77.8 0.7 all-gather.9.cloned.1.call-update
  78.5 70.9 %all-to-all-done = f32[8,384,256]{2,1,0:T(8,128)} async-done(((f32[8,384,256]{2,1,0:T(8,128)}), f32[8,384,256]{2,1,0:T(8,128)}, u32[]{:S(2)}, u32[]{:S(2)}) %all-to-all-start) | async-done | bytes 3145760 | tf_op jit(solution)/shard_map/all_to_all | solution.py:18
  149.4 2.9 reduce_sum.18
  152.2 2.4 convolution_bitcast_fusion
  154.6 11.0 %all-to-all-start.1 = ((f32[32,8,1024]{2,1,0:T(8,128)}), f32[32,8,1024]{2,1,0:T(8,128)}, u32[]{:S(2)}, u32[]{:S(2)}) async-start(f32[32,8,1024]{2,1,0:T(8,128)} %convolution_bitcast_fusion), calls=%async_computation.1 | async-start | bytes 2097152 | tf_op jit(solution)/shard_map/all_to_all | solution.py:36
  165.6 0.1 mul.78
  165.7 0.1 mul.79
  165.8 0.1 mul.70
  165.9 0.1 mul.71
  166.1 27.5 %all-to-all-done.1 = f32[32,8,1024]{2,1,0:T(8,128)} async-done(((f32[32,8,1024]{2,1,0:T(8,128)}), f32[32,8,1024]{2,1,0:T(8,128)}, u32[]{:S(2)}, u32[]{:S(2)}) %all-to-all-start.1) | async-done | bytes 1048608 | tf_op jit(solution)/shard_map/all_to_all | solution.py:36
  193.5 1.3 reduce_sum.19
  194.9 0.7 fusion.6
  195.5 0.9 broadcast_in_dim.8
  196.4 7.9 %all-to-all-start.2 = ((bf16[32,8,1024]{2,1,0:T(8,128)(2,1)}), bf16[32,8,1024]{2,1,0:T(8,128)(2,1)S(1)}, u32[]{:S(2)}, u32[]{:S(2)}) async-start(bf16[32,8,1024]{2,1,0:T(8,128)(2,1)} %broadcast_in_dim.8), calls=%async_computation.2 | async-start | bytes 1048576 | tf_op jit(solution)/shard_map/all_to_all | solution.py:18
  204.3 0.0 all-gather.7.cloned.1.call-done
  204.3 13.8 %convert_bitcast_fusion = f32[2,4,4,160,1024]{4,3,0,1,2:T(8,128)} fusion(bf16[4,4,2,160,1024]{4,3,2,1,0:T(8,128)(2,1)} %bitcast.26), kind=kLoop, calls=%fused_computation | loop fusion | flops 5242880 | bytes 31457280 | tf_op jit(solution)/shard_map/convert_element_type | solution.py:103
  218.1 16.5 %copy.25 = f32[2,4,4,160,1024]{4,3,2,1,0:T(8,128)} copy(f32[2,4,4,160,1024]{4,3,0,1,2:T(8,128)} %convert_bitcast_fusion) | data formatting | bytes 41943040 | tf_op jit(solution)/shard_map/convert_element_type | solution.py:103
  234.6 20.0 %copy.27 = f32[5120,1024]{0,1:T(8,128)} copy(f32[5120,1024]{1,0:T(8,128)} %bitcast.25) | data formatting | bytes 41943040 | tf_op jit(solution)/shard_map/convert_element_type | solution.py:103
  254.6 11.8 %fusion = bf16[5120,1024]{0,1:T(8,128)(2,1)} fusion(f32[5120,1024]{0,1:T(8,128)} %copy.27, bf16[5120,256]{1,0:T(8,128)(2,1)S(1)} %copy-done, bf16[32,8,1024]{2,1,0:T(8,128)(2,1)S(1)} %all-to-all-done.2), kind=kOutput, calls=%fused_computation.2 | convolution fusion | flops 2700083200 | bytes 34603008 | tf_op jit(solution)/shard_map/dot_general | solution.py:102
  266.4 9.5 %fusion.1 = bf16[384,1024]{0,1:T(8,128)(2,1)S(1)} fusion(bf16[5120,1024]{0,1:T(8,128)(2,1)} %fusion, bf16[384,5120]{1,0:T(8,128)(2,1)} %all-gather.9.cloned.1.call-done), kind=kOutput, calls=%fused_computation.5 | convolution fusion | flops 4026925056 | bytes 15204352 | tf_op jit(solution)/shard_map/dot_general | solution.py:105
  275.9 1.2 copy.28
  277.1 1.4 constant_dynamic-slice_fusion
  278.4 0.9 copy.29
  (18 shorter events, 0.1 us)
Async XLA Ops:
  7.2 62.0 %copy-start = (bf16[5120,256]{1,0:T(8,128)(2,1)S(1)}, bf16[5120,256]{1,0:T(8,128)(2,1)}, u32[]{:S(2)}) copy-start(bf16[5120,256]{1,0:T(8,128)(2,1)} %param.11) | copy-start | bytes 7864324
  7.2 61.9 %all-gather.5.cloned.1.call-start = ((), (), s32[]{:S(2)}) async-start(), calls=%async_computation.3 | async-start | bytes 3276800 | tf_op jit(solution)/shard_map/all_gather | solution.py:49
  29.2 175.1 %all-gather.7.cloned.1.call-start = ((), (), s32[]{:S(2)}) async-start(), calls=%async_computation.4 | async-start | bytes 13107200 | tf_op jit(solution)/shard_map/all_gather | solution.py:49
  69.1 96.5 %copy-start.4 = (s32[8,32]{1,0:T(8,128)S(1)}, s32[8,32]{1,0:T(8,128)}, u32[]{:S(2)}) copy-start(s32[8,32]{1,0:T(8,128)} %param.16) | copy-start | bytes 3076
  69.1 96.7 %copy-start.5 = (s32[8,32]{1,0:T(8,128)S(1)}, s32[8,32]{1,0:T(8,128)}, u32[]{:S(2)}) copy-start(s32[8,32]{1,0:T(8,128)} %param.14) | copy-start | bytes 3076
  69.2 125.7 %copy-start.2 = (s32[8,1024]{1,0:T(8,128)S(1)}, s32[8,1024]{1,0:T(8,128)}, u32[]{:S(2)}) copy-start(s32[8,1024]{1,0:T(8,128)} %param.15) | copy-start | bytes 98308
  69.2 125.7 %copy-start.3 = (s32[8,1024]{1,0:T(8,128)S(1)}, s32[8,1024]{1,0:T(8,128)}, u32[]{:S(2)}) copy-start(s32[8,1024]{1,0:T(8,128)} %param.13) | copy-start | bytes 98308
  72.8 79.4 %copy-start.1 = (bf16[384,1024]{1,0:T(8,128)(2,1)S(1)}, bf16[384,1024]{1,0:T(8,128)(2,1)}, u32[]{:S(2)}) copy-start(bf16[384,1024]{1,0:T(8,128)(2,1)} %param.10) | copy-start | bytes 2359300
  72.8 76.6 %all-to-all-start = ((f32[8,384,256]{2,1,0:T(8,128)}), f32[8,384,256]{2,1,0:T(8,128)}, u32[]{:S(2)}, u32[]{:S(2)}) async-start(f32[8,384,256]{2,1,0:T(8,128)} %broadcast_in_dim.7), calls=%async_computation | async-start | bytes 6291456 | tf_op jit(solution)/shard_map/all_to_all | solution.py:18
  77.7 188.7 %all-gather.9.cloned.1.call-start = ((), (), s32[]{:S(2)}) async-start(), calls=%async_computation.5 | async-start | bytes 4423680 | tf_op jit(solution)/shard_map/all_gather | solution.py:97
  154.6 39.0 %all-to-all-start.1 = ((f32[32,8,1024]{2,1,0:T(8,128)}), f32[32,8,1024]{2,1,0:T(8,128)}, u32[]{:S(2)}, u32[]{:S(2)}) async-start(f32[32,8,1024]{2,1,0:T(8,128)} %convolution_bitcast_fusion), calls=%async_computation.1 | async-start | bytes 2097152 | tf_op jit(solution)/shard_map/all_to_all | solution.py:36
  196.4 58.2 %all-to-all-start.2 = ((bf16[32,8,1024]{2,1,0:T(8,128)(2,1)}), bf16[32,8,1024]{2,1,0:T(8,128)(2,1)S(1)}, u32[]{:S(2)}, u32[]{:S(2)}) async-start(bf16[32,8,1024]{2,1,0:T(8,128)(2,1)} %broadcast_in_dim.8), calls=%async_computation.2 | async-start | bytes 1048576 | tf_op jit(solution)/shard_map/all_to_all | solution.py:18
Sparse Core Ops, SparseCore 0:
  29.3 39.7 all-gather.4
  70.9 111.1 all-gather.6
  184.0 67.3 all-gather.8
where the time goes:
time: 287 us; the launch traced here: 286 us
  waiting for transfers between devices  139 us (48%)
  local copies, waits for them, and re-layouts  43.4 us (15%)
  matrix products  25.1 us (9%)
  starting transfers between devices  23.9 us (8%)
  blocking collectives  21.9 us (8%)
  other arithmetic  18.6 us (6%)
  between operations  13.9 us (5%)
    all_to_all x2, waiting for transfers between devices, sent_to_all(): lax.all_to_all(jnp.broadcast_to(shard[None], (size, *shard.shape)), axis,...  70.9 us
    all_gather x2, waiting for transfers between devices, gather_in_order(): pieces = lax.all_gather(pieces, axes[k], axis=0, tiled=True)  39.9 us
    convert_element_type x2, local copies, waits for them, and re-layouts, body(): old_full.astype(jnp.float32) - learn_rate * delta_full  36.5 us
    all_to_all x1, waiting for transfers between devices, sum_at_owner(): lax.all_to_all(pieces, axis, split_axis=0, concat_axis=0, tiled=True)  27.5 us
    all_gather x1, blocking collectives, gather_in_order(): pieces = lax.all_gather(pieces, axes[k], axis=0, tiled=True)  21.9 us
    convert_element_type x1, other arithmetic, body(): old_full.astype(jnp.float32) - learn_rate * delta_full  13.8 us
    all_to_all x2, starting transfers between devices, sent_to_all(): lax.all_to_all(jnp.broadcast_to(shard[None], (size, *shard.shape)), axis,...  12.8 us
    dot_general x1, matrix products, body(): jnp.dot(projection, dir_full, preferred_element_type=jnp.float32)  11.8 us
  transfers between devices with their start and end apart: 6, of which 3 were waited for; matrix products, arithmetic and copies ran while one was open for 26% of the time, Pallas kernels for 0%

commit v1 on v0

--- a/solution.py
+++ b/solution.py
@@ -46,7 +46,9 @@
 def gather_in_order(shard, axes, sequence):
     pieces = shard[None]
     for k in sequence:
-        pieces = lax.all_gather(pieces, axes[k], axis=0, tiled=True)
+        pieces = jnp.concatenate(
+            lax.all_to_all(jnp.stack([pieces] * lax.axis_size(axes[k])), axes[k], 0, 0), axis=0
+        )
     block = [lax.axis_size(axes[k]) for k in reversed(sequence)]
     pieces = pieces.reshape(*block, *shard.shape)
     turned = sorted(range(len(sequence)), key=lambda place: sequence[len(sequence) - 1 - place])

time: 287 us -> 403 us (1.40)
  blocking collectives: 21.9 us -> 108 us
  waiting for transfers between devices: 139 us -> 152 us
  local copies, waits for them, and re-layouts: 43.4 us -> 53.3 us
  starting transfers between devices: 23.9 us -> 29 us
    all_to_all x1 -> x3, waiting for transfers between devices: 27.5 us -> 151 us  [gather_in_order(): lax.all_to_all(jnp.stack([pieces] * lax.axis_size(axes[k])), axes[k], 0, 0)]
    all_to_all x0 -> x2, blocking collectives: none -> 108 us  [the longest x1 74.9 us: sent_to_all(): lax.all_to_all(jnp.broadcast_to(shard[None], (size, *shard.shape)), axis,...]
    all_to_all x2 -> x1, waiting for transfers between devices: 70.9 us -> 0.01 us  [sent_to_all(): lax.all_to_all(jnp.broadcast_to(shard[None], (size, *shard.shape)), axis,...]
    all_gather x2 -> x0, waiting for transfers between devices: 39.9 us -> none  [gather_in_order(): pieces = lax.all_gather(pieces, axes[k], axis=0, tiled=True)]
    all_gather x1 -> x0, blocking collectives: 21.9 us -> none  [gather_in_order(): pieces = lax.all_gather(pieces, axes[k], axis=0, tiled=True)]
    all_to_all x1 -> x3, starting transfers between devices: 11 us -> 20.5 us  [gather_in_order(): lax.all_to_all(jnp.stack([pieces] * lax.axis_size(axes[k])), axes[k], 0, 0)]
    another operation x0 -> x2, local copies, waits for them, and re-layouts: none -> 9.07 us  [gather_in_order(): jnp.stack([pieces] * lax.axis_size(axes[k]))]
    all_to_all x2 -> x1, starting transfers between devices: 12.8 us -> 8.48 us  [sent_to_all(): lax.all_to_all(jnp.broadcast_to(shard[None], (size, *shard.shape)), axis,...]
  transfers between devices with their start and end apart: 6 -> 5, of which waited for: 3 -> 3; matrix products, arithmetic and copies ran while one was open for 26% -> 18% of each run, Pallas kernels for 0% -> 0%
where the time goes in v1:
time: 403 us; the launch traced here: 402 us
  waiting for transfers between devices  152 us (38%)
  blocking collectives  108 us (27%)
  local copies, waits for them, and re-layouts  53.3 us (13%)
  starting transfers between devices  29 us (7%)
  matrix products  26 us (6%)
  other arithmetic  19.9 us (5%)
  between operations  14.2 us (4%)
    all_to_all x3, waiting for transfers between devices, gather_in_order(): lax.all_to_all(jnp.stack([pieces] * lax.axis_size(axes[k])), axes[k], 0, 0)  151 us
    all_to_all x1, blocking collectives, sent_to_all(): lax.all_to_all(jnp.broadcast_to(shard[None], (size, *shard.shape)), axis,...  74.9 us
    convert_element_type x2, local copies, waits for them, and re-layouts, body(): old_full.astype(jnp.float32) - learn_rate * delta_full  36.3 us
    all_to_all x1, blocking collectives, sum_at_owner(): lax.all_to_all(pieces, axis, split_axis=0, concat_axis=0, tiled=True)  32.6 us
    all_to_all x3, starting transfers between devices, gather_in_order(): lax.all_to_all(jnp.stack([pieces] * lax.axis_size(axes[k])), axes[k], 0, 0)  20.5 us
    convert_element_type x1, other arithmetic, body(): old_full.astype(jnp.float32) - learn_rate * delta_full  13.7 us
    dot_general x1, matrix products, body(): jnp.dot(projection, dir_full, preferred_element_type=jnp.float32)  11.8 us
    dot_general x1, matrix products, body(): result = jnp.dot(full_next, full_weight, preferred_element_type=jnp.float32)  9.48 us
  transfers between devices with their start and end apart: 5, of which 3 were waited for; matrix products, arithmetic and copies ran while one was open for 18% of the time, Pallas kernels for 0%

profile of v1, /device:TPU:2, one launch (start us, length us, event | category | flops | bytes accessed | tf_op | source)
XLA Modules:
  0.0 401.9 jit_solution(10962381859534769749)
XLA Ops:
  7.2 2.1 pad_maximum_fusion
  9.3 8.5 %all-to-all-start = ((bf16[2,1,160,1024]{3,2,1,0:T(8,128)(2,1)}), bf16[2,1,160,1024]{3,2,1,0:T(8,128)(2,1)S(1)}, u32[]{:S(2)}, u32[]{:S(2)}) async-start(bf16[2,1,160,1024]{3,2,1,0:T(8,128)(2,1)} %pad_maximum_fusion), calls=%async_computation | async-start | bytes 1310720 | tf_op jit(solution)/shard_map/all_to_all | solution.py:50
  17.8 2.2 convolution_bitcast_fusion.1
  19.9 1.9 copy.21
  21.8 15.4 %all-to-all-done = bf16[2,1,160,1024]{3,2,1,0:T(8,128)(2,1)S(1)} async-done(((bf16[2,1,160,1024]{3,2,1,0:T(8,128)(2,1)}), bf16[2,1,160,1024]{3,2,1,0:T(8,128)(2,1)S(1)}, u32[]{:S(2)}, u32[]{:S(2)}) %all-to-all-start) | async-done | bytes 655392 | tf_op jit(solution)/shard_map/all_to_all | solution.py:50
  37.2 1.3 broadcast_in_dim.4
  38.4 74.9 %all_to_all.30 = f32[8,384,256]{2,1,0:T(8,128)} all-to-all(f32[8,384,256]{2,1,0:T(8,128)S(1)} %broadcast_in_dim.4), channel_id=1, replica_groups=mesh['col'=8,'dp_0'=2,'dp_1'=4,'dp_2'=4] {'col'}, dimensions={0} | all-to-all | bytes 6291456 | tf_op jit(solution)/shard_map/all_to_all | solution.py:18
  113.4 1.9 stack.10
  115.2 4.5 %all-to-all-start.1 = ((bf16[4,2,160,1024]{3,2,1,0:T(8,128)(2,1)}), bf16[4,2,160,1024]{3,2,1,0:T(8,128)(2,1)}, u32[]{:S(2)}, u32[]{:S(2)}) async-start(bf16[4,2,160,1024]{3,2,1,0:T(8,128)(2,1)} %stack.10), calls=%async_computation.1 | async-start | bytes 5242880 | tf_op jit(solution)/shard_map/all_to_all | solution.py:50
  119.8 2.1 reduce_sum.18
  121.9 2.6 convolution_bitcast_fusion
  124.5 27.2 %all-to-all-done.1 = bf16[4,2,160,1024]{3,2,1,0:T(8,128)(2,1)} async-done(((bf16[4,2,160,1024]{3,2,1,0:T(8,128)(2,1)}), bf16[4,2,160,1024]{3,2,1,0:T(8,128)(2,1)}, u32[]{:S(2)}, u32[]{:S(2)}) %all-to-all-start.1) | async-done | bytes 2621472 | tf_op jit(solution)/shard_map/all_to_all | solution.py:50
  151.7 32.6 %all_to_all.31 = f32[32,8,1024]{2,1,0:T(8,128)} all-to-all(f32[32,8,1024]{2,1,0:T(8,128)} %convolution_bitcast_fusion), channel_id=1, replica_groups=mesh['col'=8,'dp_0'=2,'dp_1'=4,'dp_2'=4] {'dp_0','dp_1','dp_2'}, dimensions={0} | all-to-all | bytes 2097152 | tf_op jit(solution)/shard_map/all_to_all | solution.py:36
  184.3 7.2 %stack.11 = bf16[4,8,160,1024]{3,2,1,0:T(8,128)(2,1)} broadcast(bf16[8,160,1024]{2,1,0:T(8,128)(2,1)} %bitcast.2), dimensions={1,2,3} | broadcast | bytes 13107200 | tf_op jit(solution)/shard_map/stack | solution.py:50
  191.6 7.5 %all-to-all-start.2 = ((bf16[4,8,160,1024]{3,2,1,0:T(8,128)(2,1)}), bf16[4,8,160,1024]{3,2,1,0:T(8,128)(2,1)}, u32[]{:S(2)}, u32[]{:S(2)}) async-start(bf16[4,8,160,1024]{3,2,1,0:T(8,128)(2,1)} %stack.11), calls=%async_computation.2 | async-start | bytes 20971520 | tf_op jit(solution)/shard_map/all_to_all | solution.py:50
  199.1 0.7 all-gather.2.cloned.1.call-update
  199.9 0.1 mul.79
  200.0 0.1 mul.70
  200.1 0.1 mul.71
  200.2 1.3 reduce_sum.19
  201.6 0.7 fusion.6
  202.2 108.6 %all-to-all-done.2 = bf16[4,8,160,1024]{3,2,1,0:T(8,128)(2,1)} async-done(((bf16[4,8,160,1024]{3,2,1,0:T(8,128)(2,1)}), bf16[4,8,160,1024]{3,2,1,0:T(8,128)(2,1)}, u32[]{:S(2)}, u32[]{:S(2)}) %all-to-all-start.2) | async-done | bytes 10485792 | tf_op jit(solution)/shard_map/all_to_all | solution.py:50
  310.9 0.9 broadcast_in_dim.5
  311.7 8.5 %all-to-all-start.5 = ((bf16[32,8,1024]{2,1,0:T(8,128)(2,1)}), bf16[32,8,1024]{2,1,0:T(8,128)(2,1)S(1)}, u32[]{:S(2)}, u32[]{:S(2)}) async-start(bf16[32,8,1024]{2,1,0:T(8,128)(2,1)} %broadcast_in_dim.5), calls=%async_computation.5 | async-start | bytes 1048576 | tf_op jit(solution)/shard_map/all_to_all | solution.py:18
  320.2 13.7 %convert_bitcast_fusion = f32[2,4,4,160,1024]{4,3,0,1,2:T(8,128)} fusion(bf16[4,4,2,160,1024]{4,3,2,1,0:T(8,128)(2,1)} %bitcast.11), kind=kLoop, calls=%fused_computation | loop fusion | flops 5242880 | bytes 31457280 | tf_op jit(solution)/shard_map/convert_element_type | solution.py:105
  333.9 16.4 %copy.20 = f32[2,4,4,160,1024]{4,3,2,1,0:T(8,128)} copy(f32[2,4,4,160,1024]{4,3,0,1,2:T(8,128)} %convert_bitcast_fusion) | data formatting | bytes 41943040 | tf_op jit(solution)/shard_map/convert_element_type | solution.py:105
  350.3 19.9 %copy.22 = f32[5120,1024]{0,1:T(8,128)} copy(f32[5120,1024]{1,0:T(8,128)} %bitcast.27) | data formatting | bytes 41943040 | tf_op jit(solution)/shard_map/convert_element_type | solution.py:105
  370.3 11.8 %fusion = bf16[5120,1024]{0,1:T(8,128)(2,1)} fusion(f32[5120,1024]{0,1:T(8,128)} %copy.22, bf16[5120,256]{1,0:T(8,128)(2,1)S(1)} %copy-done, bf16[32,8,1024]{2,1,0:T(8,128)(2,1)S(1)} %all-to-all-done.5), kind=kOutput, calls=%fused_computation.2 | convolution fusion | flops 2700083200 | bytes 34603008 | tf_op jit(solution)/shard_map/dot_general | solution.py:104
  382.1 9.5 %fusion.1 = bf16[384,1024]{0,1:T(8,128)(2,1)S(1)} fusion(bf16[5120,1024]{0,1:T(8,128)(2,1)} %fusion, bf16[384,5120]{1,0:T(8,128)(2,1)} %all-gather.2.cloned.1.call-done), kind=kOutput, calls=%fused_computation.5 | convolution fusion | flops 4026925056 | bytes 15204352 | tf_op jit(solution)/shard_map/dot_general | solution.py:107
  391.6 1.2 copy.23
  392.7 1.4 constant_dynamic-slice_fusion
  394.1 0.9 copy.24
  (16 shorter events, 0.1 us)
Async XLA Ops:
  7.2 10.6 %copy-start = (bf16[5120,256]{1,0:T(8,128)(2,1)S(1)}, bf16[5120,256]{1,0:T(8,128)(2,1)}, u32[]{:S(2)}) copy-start(bf16[5120,256]{1,0:T(8,128)(2,1)} %param.11) | copy-start | bytes 7864324
  9.3 27.9 %all-to-all-start = ((bf16[2,1,160,1024]{3,2,1,0:T(8,128)(2,1)}), bf16[2,1,160,1024]{3,2,1,0:T(8,128)(2,1)S(1)}, u32[]{:S(2)}, u32[]{:S(2)}) async-start(bf16[2,1,160,1024]{3,2,1,0:T(8,128)(2,1)} %pad_maximum_fusion), calls=%async_computation | async-start | bytes 1310720 | tf_op jit(solution)/shard_map/all_to_all | solution.py:50
  115.2 36.5 %all-to-all-start.1 = ((bf16[4,2,160,1024]{3,2,1,0:T(8,128)(2,1)}), bf16[4,2,160,1024]{3,2,1,0:T(8,128)(2,1)}, u32[]{:S(2)}, u32[]{:S(2)}) async-start(bf16[4,2,160,1024]{3,2,1,0:T(8,128)(2,1)} %stack.10), calls=%async_computation.1 | async-start | bytes 5242880 | tf_op jit(solution)/shard_map/all_to_all | solution.py:50
  191.5 8.2 %copy-start.3 = (s32[8,32]{1,0:T(8,128)S(1)}, s32[8,32]{1,0:T(8,128)}, u32[]{:S(2)}) copy-start(s32[8,32]{1,0:T(8,128)} %param.16) | copy-start | bytes 3076
  191.5 8.5 %copy-start.4 = (s32[8,32]{1,0:T(8,128)S(1)}, s32[8,32]{1,0:T(8,128)}, u32[]{:S(2)}) copy-start(s32[8,32]{1,0:T(8,128)} %param.14) | copy-start | bytes 3076
  191.6 10.0 %copy-start.1 = (s32[8,1024]{1,0:T(8,128)S(1)}, s32[8,1024]{1,0:T(8,128)}, u32[]{:S(2)}) copy-start(s32[8,1024]{1,0:T(8,128)} %param.15) | copy-start | bytes 98308
  191.6 10.0 %copy-start.2 = (s32[8,1024]{1,0:T(8,128)S(1)}, s32[8,1024]{1,0:T(8,128)}, u32[]{:S(2)}) copy-start(s32[8,1024]{1,0:T(8,128)} %param.13) | copy-start | bytes 98308
  191.6 119.3 %all-to-all-start.2 = ((bf16[4,8,160,1024]{3,2,1,0:T(8,128)(2,1)}), bf16[4,8,160,1024]{3,2,1,0:T(8,128)(2,1)}, u32[]{:S(2)}, u32[]{:S(2)}) async-start(bf16[4,8,160,1024]{3,2,1,0:T(8,128)(2,1)} %stack.11), calls=%async_computation.2 | async-start | bytes 20971520 | tf_op jit(solution)/shard_map/all_to_all | solution.py:50
  199.1 183.0 %all-gather.2.cloned.1.call-start = ((), (), s32[]{:S(2)}) async-start(), calls=%async_computation.6 | async-start | bytes 4423680 | tf_op jit(solution)/shard_map/all_gather | solution.py:99
  311.7 58.5 %all-to-all-start.5 = ((bf16[32,8,1024]{2,1,0:T(8,128)(2,1)}), bf16[32,8,1024]{2,1,0:T(8,128)(2,1)S(1)}, u32[]{:S(2)}, u32[]{:S(2)}) async-start(bf16[32,8,1024]{2,1,0:T(8,128)(2,1)} %broadcast_in_dim.5), calls=%async_computation.5 | async-start | bytes 1048576 | tf_op jit(solution)/shard_map/all_to_all | solution.py:18
Sparse Core Ops, SparseCore 0:
  201.6 50.0 all-gather.1
